TPU v7x, 512 devices: a whole 4x4x16 slice. The times are simulated.
512 devices in a mesh: samp: 64 (over z, x), blk: 8 (over y, core).
Axes of the slice: x: 4, y: 4, z: 16, core: 2. Of those that a mesh axis runs over, the one named last changes fastest.
Arguments:
- genotypes: bfloat16 [65536, 4000], P('samp', 'blk'), may hold values from 0 to 2, as said below
- traits: float32 [65536, 8], P('samp'), may hold values from -3000 to 3000
- observed: int32 [65536, 8], P('samp'), may hold values from 0 to 1, as said below
- fold_index: int32 [65536], P('samp'), may hold values from 0 to 4, never falling along the last dimension, each value on 1 to 26214 neighbouring positions
Outputs:
- stack_gram: float32 [8, 5, 40, 40], P('blk')
- stack_cross: float32 [8, 5, 40], P('blk')
Inputs may be any that keep to these rules, and one draw needn't show every extreme that they name: `genotypes`: genotype dosages, whole numbers. `observed`: each trait is measured in at least one sample.
All inputs are finite; a program needn't handle non-finite values.
Results may differ from a plain program's by a relative error of at most 0.0003.
Values sent between devices are 32-bit elements; how exact they have to be, the bound alone decides.
A program may use at most 64 MiB of HBM per device.

v0:
```python
import jax
import jax.numpy as jnp
from jax import lax
from jax.sharding import PartitionSpec as P

BLOCK = 500
TRAITS = 8
FOLDS = 5
HERITABILITY = (0.01, 0.25, 0.5, 0.75, 0.99)
PRECISE = lax.Precision.HIGHEST


def solve_one(lower_factor, right_side):
    return jax.scipy.linalg.cho_solve((lower_factor, True), right_side)


def body(genotypes, traits, observed, fold_index):
    local_rows, local_cols = genotypes.shape
    local_blocks = local_cols // BLOCK
    sample_devices = lax.axis_size("samp")
    block_devices = lax.axis_size("blk")
    samples = local_rows * sample_devices
    markers = local_cols * block_devices
    penalty_count = len(HERITABILITY)
    present = observed.astype(jnp.float32)
    masked = present * traits
    dosage_bf = genotypes.reshape(local_rows, local_blocks, BLOCK)
    dosage = dosage_bf.astype(jnp.float32)
    gram_local = jnp.einsum(
        "sbi,sbj->bij", dosage_bf, dosage_bf, preferred_element_type=jnp.float32
    )
    sums_local = jnp.sum(dosage, 0)
    trait_local = jnp.einsum("sbj,sp->bjp", dosage, masked, precision=PRECISE)
    present_local = jnp.einsum("sbj,sp->bjp", dosage, present, precision=PRECISE)
    counts_local = jnp.sum(present, 0)
    first_local = jnp.sum(masked, 0)
    second_local = jnp.sum(masked * traits, 0)
    gram_total, column_sums, dosage_trait, dosage_present, counts, trait_sums, trait_squares = (
        lax.psum(
            (
                gram_local,
                sums_local,
                trait_local,
                present_local,
                counts_local,
                first_local,
                second_local,
            ),
            "samp",
        )
    )
    mean_trait = trait_sums / counts
    trait_scale = jnp.sqrt(trait_squares / counts - mean_trait * mean_trait + 1e-05)
    scaled = present * (traits - mean_trait) / trait_scale
    mean_dosage = column_sums / samples
    dosage_scale = jnp.sqrt(
        jnp.diagonal(gram_total, axis1=1, axis2=2) / samples - mean_dosage * mean_dosage + 1e-05
    )
    covariance = (gram_total - column_sums[:, :, None] * column_sums[:, None, :] / samples) / (
        dosage_scale[:, :, None] * dosage_scale[:, None, :]
    )
    right_side = (
        (dosage_trait - dosage_present * mean_trait) / trait_scale / dosage_scale[:, :, None]
    )
    identity = jnp.eye(BLOCK, dtype=jnp.float32)
    fit_count = local_blocks * penalty_count
    position = lax.axis_index("samp")
    assigned = jnp.minimum(
        (position * fit_count + sample_devices - 1) // sample_devices, fit_count - 1
    )
    owning = assigned * sample_devices // fit_count == position
    fit_block = assigned // penalty_count
    fit_penalty = assigned % penalty_count
    penalty_table = jnp.array(
        [markers * (1.0 - fraction) / fraction for fraction in HERITABILITY], dtype=jnp.float32
    )
    penalty = jnp.sum(jnp.where(jnp.arange(penalty_count) == fit_penalty, penalty_table, 0.0))
    chosen_cov = lax.dynamic_index_in_dim(covariance, fit_block, 0, keepdims=False)
    chosen_side = lax.dynamic_index_in_dim(right_side, fit_block, 0, keepdims=False)
    lower_factor = jnp.linalg.cholesky(chosen_cov + penalty * identity)
    solution = solve_one(lower_factor, chosen_side)
    selector = jnp.logical_and(jnp.arange(fit_count) == assigned, owning).astype(jnp.float32)
    contribution = selector[:, None, None] * solution[None]
    coefficients = lax.psum(contribution, "samp").reshape(
        local_blocks, penalty_count, BLOCK, TRAITS
    )
    centred = (dosage - mean_dosage) / dosage_scale
    predicted = jnp.einsum("sbj,brjp->pbrs", centred, coefficients, precision=PRECISE)
    energy = lax.psum(jnp.sum(predicted * predicted, 3), "samp")
    standard = predicted / jnp.sqrt(energy / samples + 1e-06)[:, :, :, None]
    regrouped = lax.all_to_all(standard, "blk", split_axis=0, concat_axis=1, tiled=True)
    trait_share = TRAITS // block_devices
    stacked = regrouped.reshape(trait_share, -1, local_rows)
    first_trait = lax.axis_index("blk") * trait_share
    scaled_share = lax.dynamic_slice_in_dim(scaled, first_trait, trait_share, 1)
    present_share = lax.dynamic_slice_in_dim(present, first_trait, trait_share, 1)
    fold_hits = (fold_index[None, :] == jnp.arange(FOLDS, dtype=jnp.int32)[:, None]).astype(
        jnp.float32
    )
    weighting = fold_hits[:, None, :] * present_share.T[None]
    weighted = weighting[:, :, None, :] * stacked[None]
    gram_part = jnp.einsum("kpls,pms->pklm", weighted, stacked, precision=PRECISE)
    cross_part = jnp.einsum("kpls,sp->pkl", weighted, scaled_share, precision=PRECISE)
    gram_sum, cross_sum = lax.psum((gram_part, cross_part), "samp")
    factor = FOLDS / samples
    return (gram_sum * factor, cross_sum * factor)


def solution(mesh):
    in_specs = (P("samp", "blk"), P("samp", None), P("samp", None), P("samp"))
    out_specs = (P("blk", None, None, None), P("blk", None, None))
    return jax.shard_map(body, mesh=mesh, in_specs=in_specs, out_specs=out_specs, check_vma=False)
```

profile of v0, /device:TPU:8, one launch (start us, length us, event | category | flops | bytes accessed | tf_op | source)
XLA Modules:
  0.0 1162.0 jit_solution(14717013578681250181)
XLA Ops:
  7.2 3.3 convolution_bitcast_fusion
  10.6 1.1 copy-done.1
  12.0 0.9 convolution_bitcast_fusion.1
  12.9 0.6 convert_element_type.18
  13.5 0.9 convolution_bitcast_fusion.2
  14.6 285.7 %all-reduce.4 = (f32[1,500]{1,0:T(1,128)S(1)}, f32[1,500,8]{1,2,0:T(8,128)}, f32[1,500,8]{1,2,0:T(8,128)}, f32[8]{0:T(128)S(1)}, f32[8]{0:T(128)S(1)}, /*index=5*/f32[8]{0:T(128)S(1)}) all-reduce(f32[1,500]{1,0:T(1,128)S(1)} %bitcast.135, f32[1,500,8]{1,2,0:T(8,128)S(1)} %convolution_bitcast_fusion.2, ...), channel_id=1, replica_groups=mesh['samp'=64,'blk'=8] {'samp'}, use_global_device_ids=true, to_apply=%region_2.0 | all-reduce | flops 8524 | bytes 68192 | tf_op jit(solution)/shard_map/psum | solution.py:39
  300.3 0.6 copy-done.11
  300.9 0.6 dynamic-slice.3
  301.4 0.6 dynamic-slice.4
  302.0 0.6 iota_multiply_fusion
  302.6 0.5 and_convert_fusion
  303.2 0.6 fusion.72
  303.8 10.4 gather_fusion
  314.2 0.6 broadcast_multiply_fusion.4
  314.8 1.9 bitcast_add_fusion.1
  316.7 1.5 copy.16
  318.3 1.0 fusion.14
  319.3 1.0 copy-done.2
  320.3 11.7 %cholesky.104 = f32[128,128]{1,0:T(8,128)S(1)} custom-call(f32[128,128]{1,0:T(8,128)S(1)} %cholesky.269), custom_call_target="Cholesky" | custom-call | tf_op jit(solution)/shard_map/jit(cholesky)/cholesky | solution.py:80
  332.1 0.6 select_reduce_fusion.2
  332.8 9.8 custom-call.34
  342.6 0.5 constant_dynamic-update-slice_fusion.3
  343.1 0.5 convolution_subtract_fusion
  343.6 0.6 cholesky.273
  344.2 13.2 %cholesky.217 = f32[128,128]{1,0:T(8,128)} custom-call(f32[128,128]{1,0:T(8,128)} %cholesky.273), custom_call_target="Cholesky" | custom-call | tf_op jit(solution)/shard_map/jit(cholesky)/cholesky | solution.py:80
  357.4 2.0 select_reduce_fusion.1
  359.4 11.4 custom-call.35
  370.8 1.2 convolution_dynamic-update-slice_fusion
  372.0 0.4 convolution_subtract_fusion.1
  372.4 12.3 %cholesky.238 = f32[128,128]{1,0:T(8,128)} custom-call(f32[128,128]{1,0:T(8,128)S(1)} %cholesky.278), custom_call_target="Cholesky" | custom-call | tf_op jit(solution)/shard_map/jit(cholesky)/cholesky | solution.py:80
  384.7 0.9 select_reduce_fusion
  385.6 0.7 compare_reduce_fusion.1
  386.3 10.4 custom-call.36
  396.8 1.1 convolution_dynamic-update-slice_fusion.1
  397.8 0.4 convolution_subtract_fusion.2
  398.2 10.8 cholesky.258
  409.1 0.6 compare_reduce_fusion
  409.7 1.3 compare_reduce_fusion.2
  413.8 0.5 copy-done.16
  414.2 6.3 while.1
  414.3 0.6 fusion.97
  414.9 1.4 bitcast_dynamic-update-slice_fusion.2
  416.4 0.6 fusion.97
  417.0 1.4 bitcast_dynamic-update-slice_fusion.2
  418.6 0.6 fusion.97
  419.2 1.4 bitcast_dynamic-update-slice_fusion.2
  420.7 39.3 %custom-call.37 = f32[4,128,128]{1,2,0:T(8,128)S(1)} custom-call(f32[4,128,128]{2,1,0:T(8,128)S(1)} %pad_maximum_fusion), custom_call_target="InvertDiagBlocksLowerTriangular" | custom-call | tf_op jit(solution)/shard_map/jit(_cho_solve)/triangular_solve | solution.py:14
  461.1 0.3 convolution_subtract_fusion.6
  462.2 0.2 convolution_subtract_fusion.4
  462.6 0.3 convolution_subtract_fusion.3
  463.2 0.7 broadcast_multiply_fusion.1
  463.9 0.8 constant_dynamic-slice_fusion.1
  464.7 257.0 %all-reduce.10.cloned.1.call-done = f32[5,500,8]{1,2,0:T(8,128)} async-done(((f32[5,500,8]{1,2,0:T(8,128)}), f32[5,500,8]{1,2,0:T(8,128)}) %all-reduce.10.cloned.1.call-update) | async-done | bytes 80016 | tf_op jit(solution)/shard_map/psum | solution.py:84
  721.7 2.5 multiply_reduce_fusion
  724.3 139.6 %psum.88 = f32[8,1,5]{2,0,1:T(8,128)S(1)} all-reduce(f32[8,1,5]{2,0,1:T(8,128)S(1)} %bitcast.133), channel_id=1, replica_groups=mesh['samp'=64,'blk'=8] {'samp'}, use_global_device_ids=true, to_apply=%region_22.23 | all-reduce | flops 40 | bytes 320 | tf_op jit(solution)/shard_map/psum | solution.py:89
  864.2 0.8 copy.19
  865.0 4.8 all-to-all-start
  869.8 5.0 all-to-all-done
  874.8 0.4 reduce.27
  875.3 3.2 fusion.4
  878.5 0.8 fusion.11
  879.3 274.3 %all-reduce.3 = (f32[1,5,40,40]{3,2,1,0:T(8,128)S(1)}, f32[1,5,40]{2,0,1:T(1,128)S(1)}) all-reduce(f32[1,5,40,40]{3,2,1,0:T(8,128)S(1)} %fusion.11, f32[1,5,40]{2,0,1:T(1,128)S(1)} %dot_general.44), channel_id=1, replica_groups=mesh['samp'=64,'blk'=8] {'samp'}, use_global_device_ids=true, to_apply=%region_23.24 | all-reduce | flops 8200 | bytes 65600 | tf_op jit(solution)/shard_map/psum | solution.py:104
  1153.7 0.7 broadcast_multiply_fusion
  1154.3 0.6 broadcast_multiply_fusion.2
  (77 shorter events, 3.8 us)
Async XLA Ops:
  7.2 296.6 %all-reduce.8.cloned.1.call-start = ((), (), s32[]{:S(2)}) async-start(), calls=%async_computation.1 | async-start | bytes 2064384 | tf_op jit(solution)/shard_map/psum | solution.py:39
  10.5 1.2 copy-start.1
  10.5 1.5 copy-start.4
  10.5 711.2 %all-reduce.10.cloned.1.call-start = ((), (), s32[]{:S(2)}) async-start(), calls=%async_computation.2 | async-start | bytes 163840 | tf_op jit(solution)/shard_map/psum | solution.py:84
  11.7 1.8 copy-start.5
  12.0 291.2 %copy-start.15 = (f32[5]{0:T(128)S(1)}, f32[5]{0:T(128)}, u32[]{:S(2)}) copy-start(f32[5]{0:T(128)} %constant.250.clone) | copy-start | bytes 64
  300.3 0.6 copy-start.11
  300.3 1.1 copy-start.9
  303.8 11.0 copy-start
  319.3 1.0 copy-start.2
  320.3 22.3 %copy-start.3 = (f32[500,500]{1,0:T(8,128)S(1)}, f32[500,500]{1,0:T(8,128)}, u32[]{:S(2)}) copy-start(f32[500,500]{1,0:T(8,128)} %copy-done.2) | copy-start | bytes 3000004
  413.6 0.7 copy-start.16
  413.7 46.3 %copy-start.6 = (f32[1,500,8]{1,2,0:T(8,128)S(1)}, f32[1,500,8]{1,2,0:T(8,128)}, u32[]{:S(2)}) copy-start(f32[1,500,8]{1,2,0:T(8,128)} %get-tuple-element.24) | copy-start | bytes 48004
  413.7 46.3 %copy-start.7 = (f32[1,500,8]{1,2,0:T(8,128)S(1)}, f32[1,500,8]{1,2,0:T(8,128)}, u32[]{:S(2)}) copy-start(f32[1,500,8]{1,2,0:T(8,128)} %get-tuple-element.25) | copy-start | bytes 48004
  413.7 46.3 %copy-start.10 = (f32[8]{0:T(128)S(1)}, f32[8]{0:T(128)}, u32[]{:S(2)}) copy-start(f32[8]{0:T(128)} %copy-done.9) | copy-start | bytes 100
  413.7 46.3 %copy-start.12 = (f32[8]{0:T(128)S(1)}, f32[8]{0:T(128)}, u32[]{:S(2)}) copy-start(f32[8]{0:T(128)} %copy-done.11) | copy-start | bytes 100
  420.7 42.5 %copy-start.14 = (f32[5]{0:T(128)S(1)}, f32[5]{0:T(128)}, u32[]{:S(2)}) copy-start(f32[5]{0:T(128)} %and_convert_fusion) | copy-start | bytes 64
  420.7 301.0 %copy-start.13 = (f32[1,500]{1,0:T(1,128)S(1)}, f32[1,500]{1,0:T(1,128)}, u32[]{:S(2)}) copy-start(f32[1,500]{1,0:T(1,128)} %get-tuple-element.43) | copy-start | bytes 6004
  721.7 148.1 %copy-start.8 = (s32[1024]{0:T(1024)S(1)}, s32[1024]{0:T(1024)}, u32[]{:S(2)}) copy-start(s32[1024]{0:T(1024)} %param.8) | copy-start | bytes 12292
  865.0 9.8 all-to-all-start
Sparse Core Ops, SparseCore 0:
  11.4 280.3 all-reduce.7
  464.0 257.6 all-reduce.9
where the time goes:
time: 1170 us; the launch traced here: 1160 us
  blocking collectives  700 us (60%)
  waiting for transfers between devices  262 us (22%)
  other arithmetic  134 us (11%)
  local copies, waits for them, and re-layouts  25.2 us (2%)
  matrix products  18.5 us (2%)
  between operations  17.3 us (1%)
    psum x1, blocking collectives, body(): lax.psum((gram_local, sums_local, trait_local, present_local, counts_loca...  286 us
    psum x1, blocking collectives, body(): gram_sum, cross_sum = lax.psum((gram_part, cross_part), 'samp')  274 us
    psum x1, waiting for transfers between devices, body(): lax.psum(contribution, 'samp')  257 us
    psum x1, blocking collectives, body(): energy = lax.psum(jnp.sum(predicted * predicted, 3), 'samp')  140 us
    another operation x14, other arithmetic, body(): lower_factor = jnp.linalg.cholesky(chosen_cov + penalty * identity)  85.9 us
    another operation x8, other arithmetic, solve_one(): return jax.scipy.linalg.cho_solve((lower_factor, True), right_side)  40.2 us
  transfers between devices with their start and end apart: 3, of which 2 were waited for; matrix products, arithmetic and copies ran while one was open for 1% of the time, Pallas kernels for 0%

commit v1 on v0

--- a/solution.py
+++ b/solution.py
@@ -8,6 +8,11 @@
 FOLDS = 5
 HERITABILITY = (0.01, 0.25, 0.5, 0.75, 0.99)
 PRECISE = lax.Precision.HIGHEST
+
+
+def summed_here(x, axis):
+    terms = lax.all_gather(x, axis)
+    return jnp.sum(terms, axis=0)
 
 
 def solve_one(lower_factor, right_side):
@@ -86,7 +91,7 @@
     )
     centred = (dosage - mean_dosage) / dosage_scale
     predicted = jnp.einsum("sbj,brjp->pbrs", centred, coefficients, precision=PRECISE)
-    energy = lax.psum(jnp.sum(predicted * predicted, 3), "samp")
+    energy = summed_here(jnp.sum(predicted * predicted, 3), "samp")
     standard = predicted / jnp.sqrt(energy / samples + 1e-06)[:, :, :, None]
     regrouped = lax.all_to_all(standard, "blk", split_axis=0, concat_axis=1, tiled=True)
     trait_share = TRAITS // block_devices

time: 1170 us -> 1110 us (0.949)
  blocking collectives: 700 us -> 643 us
    psum x1 -> x0, blocking collectives: 140 us -> none  [body(): energy = lax.psum(jnp.sum(predicted * predicted, 3), 'samp')]
    all_gather x0 -> x1, blocking collectives: none -> 80.5 us  [summed_here(): terms = lax.all_gather(x, axis)]
where the time goes in v1:
time: 1110 us
  blocking collectives  643 us (58%)
  waiting for transfers between devices  262 us (24%)
  other arithmetic  134 us (12%)
  local copies, waits for them, and re-layouts  25.2 us (2%)
  matrix products  18.5 us (2%)
  between operations  17.3 us (2%)
    psum x1, blocking collectives, body(): lax.psum((gram_local, sums_local, trait_local, present_local, counts_loca...  286 us
    psum x1, blocking collectives, body(): gram_sum, cross_sum = lax.psum((gram_part, cross_part), 'samp')  277 us
    psum x1, waiting for transfers between devices, body(): lax.psum(contribution, 'samp')  257 us
    another operation x14, other arithmetic, body(): lower_factor = jnp.linalg.cholesky(chosen_cov + penalty * identity)  85.9 us
    all_gather x1, blocking collectives, summed_here(): terms = lax.all_gather(x, axis)  80.5 us
    another operation x8, other arithmetic, solve_one(): return jax.scipy.linalg.cho_solve((lower_factor, True), right_side)  40.2 us
  transfers between devices with their start and end apart: 3, of which 2 were waited for; matrix products, arithmetic and copies ran while one was open for 1% of the time, Pallas kernels for 0%

profile of v1, /device:TPU:8, one launch (start us, length us, event | category | flops | bytes accessed | tf_op | source)
XLA Modules:
  0.0 1105.2 jit_solution(12713014126597593145)
XLA Ops:
  7.2 3.3 convolution_bitcast_fusion
  10.6 1.1 copy-done.1
  12.0 0.9 convolution_bitcast_fusion.1
  12.9 0.6 convert_element_type.18
  13.5 0.9 convolution_bitcast_fusion.2
  14.6 285.7 %all-reduce.4 = (f32[1,500]{1,0:T(1,128)S(1)}, f32[1,500,8]{1,2,0:T(8,128)}, f32[1,500,8]{1,2,0:T(8,128)}, f32[8]{0:T(128)S(1)}, f32[8]{0:T(128)S(1)}, /*index=5*/f32[8]{0:T(128)S(1)}) all-reduce(f32[1,500]{1,0:T(1,128)S(1)} %bitcast.133, f32[1,500,8]{1,2,0:T(8,128)S(1)} %convolution_bitcast_fusion.2, ...), channel_id=1, replica_groups=mesh['samp'=64,'blk'=8] {'samp'}, use_global_device_ids=true, to_apply=%region_2.0 | all-reduce | flops 8524 | bytes 68192 | tf_op jit(solution)/shard_map/psum | solution.py:44
  300.3 0.6 copy-done.11
  300.9 0.6 dynamic-slice.3
  301.4 0.6 dynamic-slice.4
  302.0 0.6 iota_multiply_fusion
  302.6 0.5 and_convert_fusion
  303.2 0.6 fusion.72
  303.8 10.4 gather_fusion
  314.2 0.6 broadcast_multiply_fusion.4
  314.8 1.9 bitcast_add_fusion.1
  316.7 1.5 copy.14
  318.3 1.0 fusion.14
  319.3 1.0 copy-done.2
  320.3 11.7 %cholesky.104 = f32[128,128]{1,0:T(8,128)S(1)} custom-call(f32[128,128]{1,0:T(8,128)S(1)} %cholesky.269), custom_call_target="Cholesky" | custom-call | tf_op jit(solution)/shard_map/jit(cholesky)/cholesky | solution.py:85
  332.1 0.6 select_reduce_fusion.2
  332.8 9.8 custom-call.34
  342.6 0.5 constant_dynamic-update-slice_fusion.3
  343.1 0.5 convolution_subtract_fusion
  343.6 0.6 cholesky.273
  344.2 13.2 %cholesky.217 = f32[128,128]{1,0:T(8,128)} custom-call(f32[128,128]{1,0:T(8,128)} %cholesky.273), custom_call_target="Cholesky" | custom-call | tf_op jit(solution)/shard_map/jit(cholesky)/cholesky | solution.py:85
  357.4 2.0 select_reduce_fusion.1
  359.4 11.4 %custom-call.35 = f32[1,128,128]{1,2,0:T(8,128)} custom-call(f32[1,128,128]{2,1,0:T(8,128)} %get-tuple-element.37), custom_call_target="InvertDiagBlocksLowerTriangular" | custom-call | tf_op jit(solution)/shard_map/jit(cholesky)/cholesky | solution.py:85
  370.8 1.2 convolution_dynamic-update-slice_fusion
  372.0 0.4 convolution_subtract_fusion.1
  372.4 12.3 %cholesky.238 = f32[128,128]{1,0:T(8,128)} custom-call(f32[128,128]{1,0:T(8,128)S(1)} %cholesky.278), custom_call_target="Cholesky" | custom-call | tf_op jit(solution)/shard_map/jit(cholesky)/cholesky | solution.py:85
  384.7 0.9 select_reduce_fusion
  385.6 0.7 compare_reduce_fusion.1
  386.3 10.4 custom-call.36
  396.8 1.1 convolution_dynamic-update-slice_fusion.1
  397.8 0.4 convolution_subtract_fusion.2
  398.2 10.8 cholesky.258
  409.1 0.6 compare_reduce_fusion
  409.7 1.3 compare_reduce_fusion.2
  413.8 0.5 copy-done.16
  414.2 6.3 while.1
  414.3 0.6 fusion.97
  414.9 1.4 bitcast_dynamic-update-slice_fusion.2
  416.4 0.6 fusion.97
  417.0 1.4 bitcast_dynamic-update-slice_fusion.2
  418.6 0.6 fusion.97
  419.2 1.4 bitcast_dynamic-update-slice_fusion.2
  420.7 39.3 %custom-call.37 = f32[4,128,128]{1,2,0:T(8,128)S(1)} custom-call(f32[4,128,128]{2,1,0:T(8,128)S(1)} %pad_maximum_fusion), custom_call_target="InvertDiagBlocksLowerTriangular" | custom-call | tf_op jit(solution)/shard_map/jit(_cho_solve)/triangular_solve | solution.py:19
  461.1 0.3 convolution_subtract_fusion.6
  462.2 0.2 convolution_subtract_fusion.4
  462.6 0.3 convolution_subtract_fusion.3
  463.2 0.7 broadcast_multiply_fusion.1
  463.9 0.8 constant_dynamic-slice_fusion.1
  464.7 257.0 %all-reduce.10.cloned.1.call-done = f32[5,500,8]{1,2,0:T(8,128)} async-done(((f32[5,500,8]{1,2,0:T(8,128)}), f32[5,500,8]{1,2,0:T(8,128)}) %all-reduce.10.cloned.1.call-update) | async-done | bytes 80016 | tf_op jit(solution)/shard_map/psum | solution.py:89
  721.7 2.5 multiply_reduce_fusion
  724.3 80.5 %all-gather = f32[512,5]{1,0:T(8,128)S(1)} all-gather(f32[8,5]{1,0:T(8,128)S(1)} %copy.15), channel_id=2, replica_groups=mesh['samp'=64,'blk'=8] {'samp'}, dimensions={0}, use_global_device_ids=true | all-gather | bytes 10400 | tf_op jit(solution)/shard_map/all_gather | solution.py:14
  805.1 0.8 copy.17
  806.0 4.8 all-to-all-start
  810.8 5.0 all-to-all-done
  815.8 0.4 reduce.29
  816.2 3.2 fusion.4
  819.5 0.8 fusion.11
  820.3 276.6 %all-reduce.3 = (f32[1,5,40,40]{3,2,1,0:T(8,128)S(1)}, f32[1,5,40]{2,0,1:T(1,128)S(1)}) all-reduce(f32[1,5,40,40]{3,2,1,0:T(8,128)S(1)} %fusion.11, f32[1,5,40]{2,0,1:T(1,128)S(1)} %dot_general.44), channel_id=1, replica_groups=mesh['samp'=64,'blk'=8] {'samp'}, use_global_device_ids=true, to_apply=%region_23.24 | all-reduce | flops 8200 | bytes 65600 | tf_op jit(solution)/shard_map/psum | solution.py:109
  1096.9 0.7 broadcast_multiply_fusion
  1097.6 0.6 broadcast_multiply_fusion.2
  (78 shorter events, 3.9 us)
Async XLA Ops:
  7.2 296.6 %all-reduce.8.cloned.1.call-start = ((), (), s32[]{:S(2)}) async-start(), calls=%async_computation.1 | async-start | bytes 2064384 | tf_op jit(solution)/shard_map/psum | solution.py:44
  10.5 1.2 copy-start.1
  10.5 1.5 copy-start.4
  10.5 711.2 %all-reduce.10.cloned.1.call-start = ((), (), s32[]{:S(2)}) async-start(), calls=%async_computation.2 | async-start | bytes 163840 | tf_op jit(solution)/shard_map/psum | solution.py:89
  11.7 1.8 copy-start.5
  12.0 291.2 %copy-start.15 = (f32[5]{0:T(128)S(1)}, f32[5]{0:T(128)}, u32[]{:S(2)}) copy-start(f32[5]{0:T(128)} %constant.250.clone) | copy-start | bytes 64
  300.3 0.6 copy-start.11
  300.3 1.1 copy-start.9
  303.8 11.0 copy-start
  319.3 1.0 copy-start.2
  320.3 22.3 %copy-start.3 = (f32[500,500]{1,0:T(8,128)S(1)}, f32[500,500]{1,0:T(8,128)}, u32[]{:S(2)}) copy-start(f32[500,500]{1,0:T(8,128)} %copy-done.2) | copy-start | bytes 3000004
  413.6 0.7 copy-start.16
  413.7 46.3 %copy-start.6 = (f32[1,500,8]{1,2,0:T(8,128)S(1)}, f32[1,500,8]{1,2,0:T(8,128)}, u32[]{:S(2)}) copy-start(f32[1,500,8]{1,2,0:T(8,128)} %get-tuple-element.24) | copy-start | bytes 48004
  413.7 46.3 %copy-start.7 = (f32[1,500,8]{1,2,0:T(8,128)S(1)}, f32[1,500,8]{1,2,0:T(8,128)}, u32[]{:S(2)}) copy-start(f32[1,500,8]{1,2,0:T(8,128)} %get-tuple-element.25) | copy-start | bytes 48004
  413.7 46.3 %copy-start.10 = (f32[8]{0:T(128)S(1)}, f32[8]{0:T(128)}, u32[]{:S(2)}) copy-start(f32[8]{0:T(128)} %copy-done.9) | copy-start | bytes 100
  413.7 46.3 %copy-start.12 = (f32[8]{0:T(128)S(1)}, f32[8]{0:T(128)}, u32[]{:S(2)}) copy-start(f32[8]{0:T(128)} %copy-done.11) | copy-start | bytes 100
  420.7 42.5 %copy-start.14 = (f32[5]{0:T(128)S(1)}, f32[5]{0:T(128)}, u32[]{:S(2)}) copy-start(f32[5]{0:T(128)} %and_convert_fusion) | copy-start | bytes 64
  420.7 301.0 %copy-start.13 = (f32[1,500]{1,0:T(1,128)S(1)}, f32[1,500]{1,0:T(1,128)}, u32[]{:S(2)}) copy-start(f32[1,500]{1,0:T(1,128)} %get-tuple-element.43) | copy-start | bytes 6004
  724.2 86.5 %copy-start.8 = (s32[1024]{0:T(1024)S(1)}, s32[1024]{0:T(1024)}, u32[]{:S(2)}) copy-start(s32[1024]{0:T(1024)} %param.8) | copy-start | bytes 12292
  806.0 9.8 all-to-all-start
Sparse Core Ops, SparseCore 0:
  11.4 280.3 all-reduce.7
  464.0 257.6 all-reduce.9
